TPU v7x, 128 devices: a whole 4x4x4 slice. The times are simulated.
128 devices in a mesh: slab: 8 (over z_hi, x), tile: 16 (over z_lo, y, core).
Axes of the slice: x: 4, y: 4, z: 4 (z_hi: 2, z_lo: 2; z = z_hi * 2 + z_lo), core: 2. Of those that a mesh axis runs over, the one named last changes fastest.
Arguments:
- state: float32 [512, 256, 1024], P('slab', 'tile'), may hold values from -6 to 6
- coeff: float32 [512, 256, 1024], P('slab', 'tile'), may hold values from 0.04 to 0.16
- target: float32 [512, 256, 1024], P('slab', 'tile'), may hold values from -6 to 6
- control: float32 [8, 256, 1024], P('slab', 'tile'), may hold values from -6 to 6
- multiplier: float32 [8, 256, 1024], P('slab', 'tile'), may hold values from -6 to 6
Outputs:
- final_state: float32 [512, 256, 1024], P('slab', 'tile')
- adjoint_start: float32 [512, 256, 1024], P('slab', 'tile')
- new_control: float32 [8, 256, 1024], P('slab', 'tile')
- new_multiplier: float32 [8, 256, 1024], P('slab', 'tile')
All inputs are finite; a program needn't handle non-finite values.
Results may differ from a plain program's by a relative error of at most 0.00002.
Values sent between devices are 32-bit elements; how exact they have to be, the bound alone decides.
A program may use at most 128 MiB of HBM per device.

v0:
```python
import functools

import jax
import jax.numpy as jnp
from jax import lax
from jax.experimental import pallas as pl
from jax.experimental.pallas import tpu as pltpu
from jax.sharding import PartitionSpec as P

rho_step = 0.5
tau_step = 0.5
LANES = 128
SUB = 8
CHUNK = 8
MESH = pl.DeviceIdType.MESH


def kernel(cz, nx, ny, n_slab, n_tile, unroll,
           state, coeff, target, control, multiplier,
           final, adj, new_control, new_multiplier,
           sp, mp, cf, tg, above, mult, below, flux, low_trace, low_flux,
           send, recv,
           sem_state, sem_coeff, sem_target, sem_small, sem_send, sem_recv, sem_slab_send, sem_slab_recv):
    yt_n = ny // LANES
    xt_n = nx // SUB
    pitch = nx + SUB
    plane = yt_n * pitch
    chunks = cz // CHUNK
    rows_n = sp.shape[0] * plane
    s2 = sp.reshape(rows_n, LANES)
    m2 = mp.reshape(rows_n, LANES)

    slab = lax.axis_index("slab")
    tile = lax.axis_index("tile")
    has = (tile > 0, tile < n_tile - 1)
    side_dev = ((slab, jnp.maximum(tile - 1, 0)), (slab, jnp.minimum(tile + 1, n_tile - 1)))
    up = (lax.rem(slab + 1, n_slab), tile)
    down = (lax.rem(slab + n_slab - 1, n_slab), tile)

    barrier = pltpu.get_barrier_semaphore()
    for side in range(2):
        @pl.when(has[side])
        def _():
            pl.semaphore_signal(barrier, inc=1, device_id=side_dev[side], device_id_type=MESH)
    pl.semaphore_signal(barrier, inc=1, device_id=up, device_id_type=MESH)
    pl.semaphore_signal(barrier, inc=1, device_id=down, device_id_type=MESH)

    def state_copy(k, yt):
        return pltpu.make_async_copy(
            state.at[pl.ds(k * CHUNK, CHUNK), :, pl.ds(yt * LANES, LANES)],
            sp.at[pl.ds(k * CHUNK + 1, CHUNK), yt, pl.ds(SUB, nx), :],
            sem_state.at[k, yt])

    def coeff_copy(k):
        return pltpu.make_async_copy(
            coeff.at[pl.ds(k * CHUNK, CHUNK)], cf.at[pl.ds(k * CHUNK, CHUNK)], sem_coeff.at[k])

    def target_copy(k):
        return pltpu.make_async_copy(
            target.at[pl.ds(k * CHUNK, CHUNK)], tg.at[pl.ds(k * CHUNK, CHUNK)], sem_target.at[k])

    above_copy = pltpu.make_async_copy(control, above, sem_small.at[0])
    mult_copy = pltpu.make_async_copy(multiplier, mult, sem_small.at[1])

    @pl.loop(0, chunks)
    def _(k):
        for yt in range(yt_n):
            state_copy(k, yt).start()
    above_copy.start()

    @pl.loop(0, chunks)
    def _(k):
        coeff_copy(k).start()

    @pl.loop(0, chunks)
    def _(k):
        target_copy(k).start()
    mult_copy.start()

    for side in range(2):
        @pl.when(jnp.logical_not(has[side]))
        def _():
            zeros = jnp.zeros((yt_n, LANES), jnp.float32)

            @pl.loop(1, cz + 1)
            def _(z):
                for field in (s2, m2):
                    field[pl.ds(z * plane + (SUB - 1 if side == 0 else SUB + nx), yt_n, stride=pitch), :] = zeros

    pl.semaphore_wait(barrier, 2 + has[0].astype(jnp.int32) + has[1].astype(jnp.int32))

    def slab_copy(i, src, dst, dev):
        return pltpu.make_async_remote_copy(
            src_ref=src, dst_ref=dst, send_sem=sem_slab_send.at[i], recv_sem=sem_slab_recv.at[i],
            device_id=dev, device_id_type=MESH)

    below_copy = slab_copy(0, control, below, up)
    trace_copy = slab_copy(1, final.at[pl.ds(0, 1)], low_trace, down)
    flux_copy = slab_copy(2, flux, low_flux, down)
    below_copy.start()

    def edge_copy(stage, side, k):
        return pltpu.make_async_remote_copy(
            src_ref=send.at[stage, side, pl.ds(k * CHUNK, CHUNK)],
            dst_ref=recv.at[stage, 1 - side, pl.ds(k * CHUNK, CHUNK)],
            send_sem=sem_send.at[stage, side, k], recv_sem=sem_recv.at[stage, 1 - side, k],
            device_id=side_dev[side], device_id_type=MESH)

    def send_edges(field, stage, k):
        @pl.loop(0, CHUNK)
        def _(i):
            z = k * CHUNK + i
            base = (z + 1) * plane
            send[stage, 0, z] = field[pl.ds(base + SUB, yt_n, stride=pitch), :]
            send[stage, 1, z] = field[pl.ds(base + SUB + nx - 1, yt_n, stride=pitch), :]
        for side in range(2):
            @pl.when(has[side])
            def _():
                edge_copy(stage, side, k).start()

    def take_halo(field, stage, k):
        for side in range(2):
            @pl.when(has[side])
            def _():
                edge_copy(stage, 1 - side, k).wait_recv()

                @pl.loop(0, CHUNK)
                def _(i):
                    z = k * CHUNK + i
                    base = (z + 1) * plane
                    row = SUB - 1 if side == 0 else SUB + nx
                    field[pl.ds(base + row, yt_n, stride=pitch), :] = recv[stage, side, z]

    lane = lax.broadcasted_iota(jnp.int32, (SUB, LANES), 1)
    first = lane == 0
    last = lane == LANES - 1
    zero = jnp.zeros((SUB, LANES), jnp.float32)

    def sweep(field, z, xt):
        base = (z + 1) * plane + SUB + xt * SUB
        mid = [field[pl.ds(base + yt * pitch, SUB), :] for yt in range(yt_n)]
        right = [pltpu.roll(v, 1, 1) for v in mid]
        left = [pltpu.roll(v, LANES - 1, 1) for v in mid]
        laps = []
        for yt in range(yt_n):
            at = base + yt * pitch
            y_minus = jnp.where(first, right[yt - 1] if yt else zero, right[yt])
            y_plus = jnp.where(last, left[yt + 1] if yt + 1 < yt_n else zero, left[yt])
            z_sum = field[pl.ds(at + plane, SUB), :] + field[pl.ds(at - plane, SUB), :]
            x_sum = field[pl.ds(at + 1, SUB), :] + field[pl.ds(at - 1, SUB), :]
            laps.append((z_sum + x_sum) + (y_minus + y_plus) - 6.0 * mid[yt])
        return mid, laps

    def planes(body):
        def run(k):
            @pl.loop(0, CHUNK, unroll=unroll)
            def _(i):
                body(k * CHUNK + i)
        return run

    def put(field, z, xt, yt, value):
        field[pl.ds((z + 1) * plane + SUB + xt * SUB + yt * pitch, SUB), :] = value

    def at(xt, yt):
        return pl.ds(xt * SUB, SUB), pl.ds(yt * LANES, LANES)

    @pl.loop(0, chunks)
    def _(k):
        for yt in range(yt_n):
            state_copy(k, yt).wait()
        send_edges(s2, 0, k)

    above_copy.wait()
    below_copy.wait_recv()
    for xt in range(xt_n):
        for yt in range(yt_n):
            lo = below[(0,) + at(xt, yt)]
            hi = above[(0,) + at(xt, yt)]
            for field in (s2, m2):
                put(field, -1, xt, yt, lo)
                put(field, cz, xt, yt, hi)

    @planes
    def middle(z):
        for xt in range(xt_n):
            mid, laps = sweep(s2, z, xt)
            for yt in range(yt_n):
                put(m2, z, xt, yt, mid[yt] + cf[(z,) + at(xt, yt)] * laps[yt])

    @pl.loop(0, chunks)
    def _(k):
        coeff_copy(k).wait()
        take_halo(s2, 0, k)
        middle(k)
        send_edges(m2, 1, k)

    for xt in range(xt_n):
        for yt in range(yt_n):
            put(s2, -1, xt, yt, zero)
            put(s2, cz, xt, yt, zero)

    @planes
    def finish(z):
        for xt in range(xt_n):
            mid, laps = sweep(m2, z, xt)
            for yt in range(yt_n):
                here = (z,) + at(xt, yt)
                c = cf[here]
                f = mid[yt] + c * laps[yt]
                final[here] = f
                two = f - tg[here]
                tg[here] = two
                put(s2, z, xt, yt, c * two)

    @pl.loop(0, chunks)
    def _(k):
        target_copy(k).wait()
        take_halo(m2, 1, k)
        finish(k)
        send_edges(s2, 2, k)

        @pl.when(k == 0)
        def _():
            trace_copy.start()

    for xt in range(xt_n):
        for yt in range(yt_n):
            put(m2, -1, xt, yt, zero)
            put(m2, cz, xt, yt, zero)

    mult_copy.wait()
    flux[0] = tg[0]
    new_control[0] = tg[cz - 1]

    @planes
    def back_one(z):
        for xt in range(xt_n):
            mid, laps = sweep(s2, z, xt)
            for yt in range(yt_n):
                here = (z,) + at(xt, yt)
                one = tg[here] + laps[yt]
                tg[here] = one
                put(m2, z, xt, yt, cf[here] * one)

    @pl.loop(0, chunks)
    def _(k):
        take_halo(s2, 2, k)
        back_one(k)
        send_edges(m2, 3, k)

        @pl.when(k == 0)
        def _():
            flux[0] = cf[0] * (tg[0] + flux[0])
            flux_copy.start()

    @planes
    def back_two(z):
        for xt in range(xt_n):
            mid, laps = sweep(m2, z, xt)
            for yt in range(yt_n):
                here = (z,) + at(xt, yt)
                adj[here] = tg[here] + laps[yt]

    @pl.loop(0, chunks)
    def _(k):
        take_halo(m2, 3, k)
        back_two(k)

    trace_copy.wait_recv()
    flux_copy.wait_recv()
    nm = mult[0] + rho_step * (final[cz - 1] - low_trace[0])
    new_multiplier[0] = nm
    grad = cf[cz - 1] * (tg[cz - 1] + new_control[0]) + low_flux[0]
    new_control[0] = (above[0] - tau_step * (grad + nm)) / (1.0 + tau_step)

    below_copy.wait_send()
    trace_copy.wait_send()
    flux_copy.wait_send()
    for side in range(2):
        @pl.when(has[side])
        def _():
            for stage in range(4):
                @pl.loop(0, chunks)
                def _(k):
                    edge_copy(stage, side, k).wait_send()


def iterate(n_slab, n_tile, state, coeff, target, control, multiplier, interpret=False, unroll=1):
    cz, nx, ny = state.shape
    yt_n = ny // LANES
    chunks = cz // CHUNK
    f32 = jnp.float32
    full = jax.ShapeDtypeStruct((cz, nx, ny), f32)
    face = jax.ShapeDtypeStruct((1, nx, ny), f32)
    padded = pltpu.VMEM((cz + 3, yt_n, nx + SUB, LANES), f32)
    natural = pltpu.VMEM((cz, nx, ny), f32)
    sheet = pltpu.VMEM((1, nx, ny), f32)
    edges = pltpu.VMEM((4, 2, cz, yt_n, LANES), f32)
    dma = pltpu.SemaphoreType.DMA
    return pl.pallas_call(
        functools.partial(kernel, cz, nx, ny, n_slab, n_tile, unroll),
        out_shape=(full, full, face, face),
        in_specs=[pl.BlockSpec(memory_space=pl.ANY)] * 5,
        out_specs=[pl.BlockSpec(memory_space=pltpu.VMEM)] * 4,
        scratch_shapes=[padded, padded, natural, natural] + [sheet] * 6 + [edges, edges]
        + [dma((chunks, yt_n)), dma((chunks,)), dma((chunks,)), dma((2,)),
           dma((4, 2, chunks)), dma((4, 2, chunks)), dma((3,)), dma((3,))],
        compiler_params=pltpu.CompilerParams(
            collective_id=0, has_side_effects=True, vmem_limit_bytes=56 * 2**20),
        interpret=interpret,
    )(state, coeff, target, control, multiplier)


def solution(mesh):
    spec = P("slab", "tile", None)
    run = functools.partial(iterate, mesh.shape["slab"], mesh.shape["tile"])
    return jax.shard_map(run, mesh=mesh, in_specs=(spec,) * 5, out_specs=(spec,) * 4, check_vma=False)
```

profile of v0, /device:TPU:1, one launch (start us, length us, event | category | flops | bytes accessed | tf_op | source)
XLA Modules:
  0.0 59.4 jit_solution(3166661221622477836)
XLA Ops:
  0.6 50.6 %shard_map.84 = (f32[64,16,1024]{2,1,0:T(8,128)}, f32[64,16,1024]{2,1,0:T(8,128)}, f32[1,16,1024]{2,1,0:T(8,128)}, f32[1,16,1024]{2,1,0:T(8,128)}) custom-call(f32[64,16,1024]{2,1,0:T(8,128)} %state.1, f32[64,16,1024]{2,1,0:T(8,128)} %coeff.1, f32[64,16,1024]{2,1,0:T(8,128)} %target.1, f32[1,16,1024]{2,1,0:T(8,128)} %control.1, f32[1,16,1024]{2,1,0:T(8,128)} %multiplier.1), custom_call_target="tpu_custom_call" | custom-call | tf_op jit(solution)/shard_map/pallas_call | solution.py:300
  51.2 0.0 copy-start
  51.2 4.9 %copy.13 = f32[64,16,1024]{2,1,0:T(8,128)} copy(f32[64,16,1024]{2,1,0:T(8,128)} %get-tuple-element.8) | data formatting | bytes 8388608
  56.2 0.0 copy-done
  56.2 0.0 copy-start.2
  56.2 0.0 copy-start.1
  56.2 2.0 %copy.14 = f32[64,16,1024]{2,1,0:T(8,128)} copy(f32[64,16,1024]{2,1,0:T(8,128)S(1)} %copy-done) | data formatting | bytes 8388608
  58.2 0.0 copy-done.2
  58.2 0.6 %copy.15 = f32[1,16,1024]{2,1,0:T(8,128)} copy(f32[1,16,1024]{2,1,0:T(8,128)S(1)} %copy-done.2) | data formatting | bytes 131072
  58.8 0.0 copy-done.1
  58.8 0.6 %copy.16 = f32[1,16,1024]{2,1,0:T(8,128)} copy(f32[1,16,1024]{2,1,0:T(8,128)S(1)} %copy-done.1) | data formatting | bytes 131072
Async XLA Ops:
  51.2 5.0 %copy-start = (f32[64,16,1024]{2,1,0:T(8,128)S(1)}, f32[64,16,1024]{2,1,0:T(8,128)}, u32[]{:S(2)}) copy-start(f32[64,16,1024]{2,1,0:T(8,128)} %get-tuple-element.9) | copy-start | bytes 12582916
  56.2 2.0 %copy-start.2 = (f32[1,16,1024]{2,1,0:T(8,128)S(1)}, f32[1,16,1024]{2,1,0:T(8,128)}, u32[]{:S(2)}) copy-start(f32[1,16,1024]{2,1,0:T(8,128)} %get-tuple-element.10) | copy-start | bytes 196612
  56.2 2.7 %copy-start.1 = (f32[1,16,1024]{2,1,0:T(8,128)S(1)}, f32[1,16,1024]{2,1,0:T(8,128)}, u32[]{:S(2)}) copy-start(f32[1,16,1024]{2,1,0:T(8,128)} %get-tuple-element.11) | copy-start | bytes 196612
where the time goes:
time: 59.5 us; the launch traced here: 59.4 us
  Pallas kernels  50.6 us (85%)
  local copies, waits for them, and re-layouts  8.22 us (14%)
  between operations  0.65 us (1%)
    pallas_call x1, Pallas kernels, iterate(): pl.pallas_call(functools.partial(kernel, cz, nx, ny, n_slab, n_tile, unro...  50.6 us
    unnamed x10, local copies, waits for them, and re-layouts  8.22 us

commit v1 on v0

v1 whole, which is shorter than its diff:
```python
import functools

import jax
import jax.numpy as jnp
from jax import lax
from jax.experimental import pallas as pl
from jax.experimental.pallas import tpu as pltpu
from jax.sharding import PartitionSpec as P

rho_step = 0.5
tau_step = 0.5
LANES = 128
SUB = 8
CHUNK = 16
UNROLL = 4
PARTS = 4
MESH = pl.DeviceIdType.MESH


def kernel(cz, nx, ny, n_slab, n_tile,
           state, coeff, target, control, multiplier,
           final, adj, new_control, new_multiplier,
           sp, mp, cf, tg, above, mult, below, flux, top_two, low_trace, low_flux,
           send, recv,
           sem_state, sem_coeff, sem_target, sem_small, sem_send, sem_recv, sem_slab_send, sem_slab_recv):
    yt_n = ny // LANES
    xt_n = nx // SUB
    pitch = nx + SUB
    plane = yt_n * pitch
    chunks = cz // CHUNK
    rows_n = sp.shape[0] * plane
    s2 = sp.reshape(rows_n, LANES)
    m2 = mp.reshape(rows_n, LANES)

    slab = lax.axis_index("slab")
    tile = lax.axis_index("tile")
    has = (tile > 0, tile < n_tile - 1)
    side_dev = ((slab, jnp.maximum(tile - 1, 0)), (slab, jnp.minimum(tile + 1, n_tile - 1)))
    up = (lax.rem(slab + 1, n_slab), tile)
    down = (lax.rem(slab + n_slab - 1, n_slab), tile)

    barrier = pltpu.get_barrier_semaphore()
    for side in range(2):
        @pl.when(has[side])
        def _():
            pl.semaphore_signal(barrier, inc=1, device_id=side_dev[side], device_id_type=MESH)
    pl.semaphore_signal(barrier, inc=1, device_id=up, device_id_type=MESH)
    pl.semaphore_signal(barrier, inc=1, device_id=down, device_id_type=MESH)

    def state_copy(k, yt):
        return pltpu.make_async_copy(
            state.at[pl.ds(k * CHUNK, CHUNK), :, pl.ds(yt * LANES, LANES)],
            sp.at[pl.ds(k * CHUNK + 1, CHUNK), yt, pl.ds(SUB, nx), :],
            sem_state.at[k, yt])

    def coeff_copy(k):
        return pltpu.make_async_copy(
            coeff.at[pl.ds(k * CHUNK, CHUNK)], cf.at[pl.ds(k * CHUNK, CHUNK)], sem_coeff.at[k])

    def target_copy(k):
        return pltpu.make_async_copy(
            target.at[pl.ds(k * CHUNK, CHUNK)], tg.at[pl.ds(k * CHUNK, CHUNK)], sem_target.at[k])

    above_copy = pltpu.make_async_copy(control, above, sem_small.at[0])
    mult_copy = pltpu.make_async_copy(multiplier, mult, sem_small.at[1])

    @pl.loop(0, chunks)
    def _(k):
        for yt in range(yt_n):
            state_copy(k, yt).start()
    above_copy.start()

    @pl.loop(0, chunks)
    def _(k):
        coeff_copy(k).start()

    @pl.loop(0, chunks)
    def _(k):
        target_copy(k).start()
    mult_copy.start()

    for side in range(2):
        @pl.when(jnp.logical_not(has[side]))
        def _():
            @pl.loop(0, cz)
            def _(z):
                for stage in range(4):
                    recv[stage, side, z] = jnp.zeros((yt_n, LANES), jnp.float32)

    pl.semaphore_wait(barrier, 2 + has[0].astype(jnp.int32) + has[1].astype(jnp.int32))

    def slab_copy(i, src, dst, dev):
        return pltpu.make_async_remote_copy(
            src_ref=src, dst_ref=dst, send_sem=sem_slab_send.at[i], recv_sem=sem_slab_recv.at[i],
            device_id=dev, device_id_type=MESH)

    below_copy = slab_copy(0, control, below, up)
    trace_copy = slab_copy(1, final.at[pl.ds(0, 1)], low_trace, down)
    flux_copy = slab_copy(2, flux, low_flux, down)
    below_copy.start()

    def edge_copy(stage, side, k):
        return pltpu.make_async_remote_copy(
            src_ref=send.at[stage, side, pl.ds(k * CHUNK, CHUNK)],
            dst_ref=recv.at[stage, 1 - side, pl.ds(k * CHUNK, CHUNK)],
            send_sem=sem_send.at[stage, side, k], recv_sem=sem_recv.at[stage, 1 - side, k],
            device_id=side_dev[side], device_id_type=MESH)

    def pack_edges(field, stage, z):
        base = (z + 1) * plane
        send[stage, 0, z] = field[pl.ds(base + SUB, yt_n, stride=pitch), :]
        send[stage, 1, z] = field[pl.ds(base + SUB + nx - 1, yt_n, stride=pitch), :]

    def send_edges(stage, k):
        for side in range(2):
            @pl.when(has[side])
            def _():
                edge_copy(stage, side, k).start()

    def wait_halo(stage, k):
        for side in range(2):
            @pl.when(has[side])
            def _():
                edge_copy(stage, 1 - side, k).wait_recv()

    def place_halo(field, stage, z):
        base = (z + 1) * plane
        field[pl.ds(base + SUB - 1, yt_n, stride=pitch), :] = recv[stage, 0, z]
        field[pl.ds(base + SUB + nx, yt_n, stride=pitch), :] = recv[stage, 1, z]

    lane = lax.broadcasted_iota(jnp.int32, (SUB, LANES), 1)
    first = lane == 0
    last = lane == LANES - 1
    zero = jnp.zeros((SUB, LANES), jnp.float32)

    def y_sums(field, z, xt):
        base = (z + 1) * plane + SUB + xt * SUB
        mid = [field[pl.ds(base + yt * pitch, SUB), :] for yt in range(yt_n)]
        right = [pltpu.roll(v, 1, 1) for v in mid]
        left = [pltpu.roll(v, LANES - 1, 1) for v in mid]
        return [jnp.where(first, right[yt - 1] if yt else zero, right[yt])
                + jnp.where(last, left[yt + 1] if yt + 1 < yt_n else zero, left[yt]) for yt in range(yt_n)]

    def center_and_lap(field, z, xt, yt, y_sum):
        at = (z + 1) * plane + SUB + xt * SUB + yt * pitch
        mid = field[pl.ds(at, SUB), :]
        z_sum = field[pl.ds(at + plane, SUB), :] + field[pl.ds(at - plane, SUB), :]
        x_sum = field[pl.ds(at + 1, SUB), :] + field[pl.ds(at - 1, SUB), :]
        return mid, (z_sum + x_sum) + y_sum - 6.0 * mid

    def put(field, z, xt, yt, value):
        field[pl.ds((z + 1) * plane + SUB + xt * SUB + yt * pitch, SUB), :] = value

    def at(xt, yt):
        return pl.ds(xt * SUB, SUB), pl.ds(yt * LANES, LANES)

    def sweep(field, stage_in, emit, before, after, out=None, stage_out=None):
        def one_plane(z, sums):
            place_halo(field, stage_in, z)
            for xt in range(xt_n):
                ahead = y_sums(field, z, xt + 1) if xt + 1 < xt_n else y_sums(field, z + 1, 0)
                for yt in range(yt_n):
                    emit(z, xt, yt, *center_and_lap(field, z, xt, yt, sums[yt]))
                sums = ahead
            if out is not None:
                pack_edges(out, stage_out, z)
            return sums

        def one_chunk(k, sums):
            before(k)
            wait_halo(stage_in, k)
            sums = lax.fori_loop(0, CHUNK, lambda i, c: one_plane(k * CHUNK + i, c), sums, unroll=UNROLL)
            if out is not None:
                send_edges(stage_out, k)
            after(k)
            return sums

        lax.fori_loop(0, chunks, one_chunk, y_sums(field, 0, 0))

    def nothing(k):
        pass

    @pl.loop(0, chunks)
    def _(k):
        for yt in range(yt_n):
            state_copy(k, yt).wait()

        @pl.loop(0, CHUNK, unroll=4)
        def _(i):
            pack_edges(s2, 0, k * CHUNK + i)
        send_edges(0, k)

    above_copy.wait()
    below_copy.wait_recv()
    for xt in range(xt_n):
        for yt in range(yt_n):
            lo = below[(0,) + at(xt, yt)]
            hi = above[(0,) + at(xt, yt)]
            for field in (s2, m2):
                put(field, -1, xt, yt, lo)
                put(field, cz, xt, yt, hi)

    def middle(z, xt, yt, mid, lap):
        put(m2, z, xt, yt, mid + cf[(z,) + at(xt, yt)] * lap)

    sweep(s2, 0, middle, lambda k: coeff_copy(k).wait(), nothing, m2, 1)

    for xt in range(xt_n):
        for yt in range(yt_n):
            put(s2, -1, xt, yt, zero)
            put(s2, cz, xt, yt, zero)

    def finish(z, xt, yt, mid, lap):
        here = (z,) + at(xt, yt)
        c = cf[here]
        f = mid + c * lap
        final[here] = f
        two = f - tg[here]
        tg[here] = two
        put(s2, z, xt, yt, c * two)

    def send_trace(k):
        @pl.when(k == 0)
        def _():
            trace_copy.start()

    sweep(m2, 1, finish, lambda k: target_copy(k).wait(), send_trace, s2, 2)

    for xt in range(xt_n):
        for yt in range(yt_n):
            put(m2, -1, xt, yt, zero)
            put(m2, cz, xt, yt, zero)

    flux[0] = tg[0]
    top_two[0] = tg[cz - 1]

    def back_one(z, xt, yt, mid, lap):
        here = (z,) + at(xt, yt)
        one = tg[here] + lap
        tg[here] = one
        put(m2, z, xt, yt, cf[here] * one)

    def send_flux(k):
        @pl.when(k == 0)
        def _():
            flux[0] = cf[0] * (tg[0] + flux[0])
            flux_copy.start()

    sweep(s2, 2, back_one, nothing, send_flux, m2, 3)

    def back_two(z, xt, yt, mid, lap):
        here = (z,) + at(xt, yt)
        adj[here] = tg[here] + lap

    sweep(m2, 3, back_two, nothing, nothing)

    mult_copy.wait()
    trace_copy.wait_recv()
    flux_copy.wait_recv()
    nm = mult[0] + rho_step * (final[cz - 1] - low_trace[0])
    new_multiplier[0] = nm
    grad = cf[cz - 1] * (tg[cz - 1] + top_two[0]) + low_flux[0]
    new_control[0] = (above[0] - tau_step * (grad + nm)) / (1.0 + tau_step)

    below_copy.wait_send()
    trace_copy.wait_send()
    flux_copy.wait_send()
    for side in range(2):
        @pl.when(has[side])
        def _():
            for stage in range(4):
                @pl.loop(0, chunks)
                def _(k):
                    edge_copy(stage, side, k).wait_send()


def write_out(parts, *refs):
    sem = refs[-1]
    n = (len(refs) - 1) // 2
    copies = []
    for i in range(n):
        planes = refs[i].shape[0]
        step = max(planes // parts, 1)
        for j in range(planes // step):
            span = pl.ds(j * step, step)
            copies.append(pltpu.make_async_copy(refs[i].at[span], refs[n + i].at[span], sem.at[i, j]))
    for copy in copies:
        copy.start()
    for copy in copies:
        copy.wait()


def iterate(n_slab, n_tile, state, coeff, target, control, multiplier):
    cz, nx, ny = state.shape
    yt_n = ny // LANES
    chunks = cz // CHUNK
    f32 = jnp.float32
    padded = pltpu.VMEM((cz + 3, yt_n, nx + SUB, LANES), f32)
    natural = pltpu.VMEM((cz, nx, ny), f32)
    sheet = pltpu.VMEM((1, nx, ny), f32)
    edges = pltpu.VMEM((4, 2, cz, yt_n, LANES), f32)
    dma = pltpu.SemaphoreType.DMA
    arrays = [pltpu.with_memory_space_constraint(a, pltpu.HBM) for a in (state, coeff, target, control, multiplier)]
    results = pl.pallas_call(
        functools.partial(kernel, cz, nx, ny, n_slab, n_tile),
        out_shape=(natural, natural, sheet, sheet),
        in_specs=[pl.BlockSpec(memory_space=pltpu.HBM)] * 5,
        out_specs=[pl.BlockSpec(memory_space=pltpu.VMEM)] * 4,
        scratch_shapes=[padded, padded, natural, natural] + [sheet] * 7 + [edges, edges]
        + [dma((chunks, yt_n)), dma((chunks,)), dma((chunks,)), dma((2,)),
           dma((4, 2, chunks)), dma((4, 2, chunks)), dma((3,)), dma((3,))],
        compiler_params=pltpu.CompilerParams(
            collective_id=0, has_side_effects=True, vmem_limit_bytes=40 * 2**20),
    )(*arrays)
    full = jax.ShapeDtypeStruct((cz, nx, ny), f32)
    face = jax.ShapeDtypeStruct((1, nx, ny), f32)
    return pl.pallas_call(
        functools.partial(write_out, PARTS),
        out_shape=(full, full, face, face),
        in_specs=[pl.BlockSpec(memory_space=pltpu.VMEM)] * 4,
        out_specs=[pl.BlockSpec(memory_space=pl.ANY)] * 4,
        scratch_shapes=[dma((4, PARTS))],
        compiler_params=pltpu.CompilerParams(vmem_limit_bytes=16 * 2**20),
    )(*results)


def solution(mesh):
    spec = P("slab", "tile", None)
    run = functools.partial(iterate, mesh.shape["slab"], mesh.shape["tile"])
    return jax.shard_map(run, mesh=mesh, in_specs=(spec,) * 5, out_specs=(spec,) * 4, check_vma=False)
```

time: 59.5 us -> 33.6 us (0.56)
  the two profiles are of different devices: /device:TPU:1 before, /device:TPU:32 now
where the time goes in v1:
time: 33.6 us; the launch traced here: 33.5 us
  Pallas kernels  32.9 us (98%)
  between operations  0.64 us (2%)
    pallas_call x1, Pallas kernels, iterate(): pl.pallas_call(functools.partial(kernel, cz, nx, ny, n_slab, n_tile), out...  29.5 us
    pallas_call x1, Pallas kernels, iterate(): pl.pallas_call(functools.partial(write_out, PARTS), out_shape=(full, full...  3.45 us

profile of v1, /device:TPU:32, one launch (start us, length us, event | category | flops | bytes accessed | tf_op | source)
XLA Modules:
  0.0 33.5 jit_solution(3627450407473688134)
XLA Ops:
  0.6 29.5 %shard_map.84 = (f32[64,16,1024]{2,1,0:T(8,128)S(1)}, f32[64,16,1024]{2,1,0:T(8,128)S(1)}, f32[1,16,1024]{2,1,0:T(8,128)S(1)}, f32[1,16,1024]{2,1,0:T(8,128)S(1)}) custom-call(f32[64,16,1024]{2,1,0:T(8,128)} %state.1, f32[64,16,1024]{2,1,0:T(8,128)} %coeff.1, f32[64,16,1024]{2,1,0:T(8,128)} %target.1, f32[1,16,1024]{2,1,0:T(8,128)} %control.1, ...), custom_call_target="tpu_custom_call" | custom-call | tf_op jit(solution)/shard_map/pallas_call | solution.py:304
  30.1 3.4 %shard_map.85 = (f32[64,16,1024]{2,1,0:T(8,128)}, f32[64,16,1024]{2,1,0:T(8,128)}, f32[1,16,1024]{2,1,0:T(8,128)}, f32[1,16,1024]{2,1,0:T(8,128)}) custom-call(f32[64,16,1024]{2,1,0:T(8,128)S(1)} %get-tuple-element.8.refs_0_, f32[64,16,1024]{2,1,0:T(8,128)S(1)} %get-tuple-element.9.refs_1_, f32[1,16,1024]{2,1,0:T(8,128)S(1)} %get-tuple-element.10.refs_2_, ...), custom_call_target="tpu_custom_call" | custom-call | tf_op jit(solution)/shard_map/pallas_call | solution.py:317

commit v2 on v1

--- a/solution.py
+++ b/solution.py
@@ -12,7 +12,8 @@
 LANES = 128
 SUB = 8
 CHUNK = 16
-UNROLL = 4
+GROUP = 4
+BY_DOT = 2
 PARTS = 4
 MESH = pl.DeviceIdType.MESH
 
@@ -21,7 +22,7 @@
            state, coeff, target, control, multiplier,
            final, adj, new_control, new_multiplier,
            sp, mp, cf, tg, above, mult, below, flux, top_two, low_trace, low_flux,
-           send, recv,
+           send, recv, band, dots_a, dots_b,
            sem_state, sem_coeff, sem_target, sem_small, sem_send, sem_recv, sem_slab_send, sem_slab_recv):
     yt_n = ny // LANES
     xt_n = nx // SUB
@@ -141,12 +142,23 @@
         return [jnp.where(first, right[yt - 1] if yt else zero, right[yt])
                 + jnp.where(last, left[yt + 1] if yt + 1 < yt_n else zero, left[yt]) for yt in range(yt_n)]
 
-    def center_and_lap(field, z, xt, yt, y_sum):
-        at = (z + 1) * plane + SUB + xt * SUB + yt * pitch
-        mid = field[pl.ds(at, SUB), :]
-        z_sum = field[pl.ds(at + plane, SUB), :] + field[pl.ds(at - plane, SUB), :]
-        x_sum = field[pl.ds(at + 1, SUB), :] + field[pl.ds(at - 1, SUB), :]
-        return mid, (z_sum + x_sum) + y_sum - 6.0 * mid
+    row = lax.rem(lax.broadcasted_iota(jnp.int32, (2 * LANES, LANES), 0), LANES)
+    col = lax.broadcasted_iota(jnp.int32, (2 * LANES, LANES), 1)
+    swap = jnp.logical_or(jnp.logical_and(row == LANES - 1, col == 0), jnp.logical_and(row == 0, col == LANES - 1))
+    band[:, pl.ds(0, LANES)] = jnp.where(jnp.abs(row - col) == 1, 1.0, 0.0).astype(jnp.bfloat16)
+    band[:, pl.ds(LANES, LANES)] = jnp.where(swap, 1.0, 0.0).astype(jnp.bfloat16)
+    lower_half = lane < LANES // 2
+
+    def dot_sums(field, z, to):
+        rows = []
+        for p in range(BY_DOT):
+            base = (z + p + 1) * plane + SUB
+            for yt in range(yt_n):
+                mid = field[pl.ds(base + yt * pitch, nx), :]
+                high = mid.astype(jnp.bfloat16)
+                low = (mid - high.astype(jnp.float32)).astype(jnp.bfloat16)
+                rows.append(jnp.concatenate([high, low], axis=1))
+        to[...] = jnp.dot(jnp.concatenate(rows, axis=0), band[...], preferred_element_type=jnp.float32)
 
     def put(field, z, xt, yt, value):
         field[pl.ds((z + 1) * plane + SUB + xt * SUB + yt * pitch, SUB), :] = value
@@ -154,28 +166,51 @@
     def at(xt, yt):
         return pl.ds(xt * SUB, SUB), pl.ds(yt * LANES, LANES)
 
+    groups = cz // GROUP
+
     def sweep(field, stage_in, emit, before, after, out=None, stage_out=None):
-        def one_plane(z, sums):
-            place_halo(field, stage_in, z)
+        def one_group(g, have, make):
+            z = g * GROUP
+            for p in range(GROUP):
+                place_halo(field, stage_in, z + p)
+            dot_sums(field, lax.rem(g + 1, groups) * GROUP, make)
             for xt in range(xt_n):
-                ahead = y_sums(field, z, xt + 1) if xt + 1 < xt_n else y_sums(field, z + 1, 0)
+                rolled = {p: y_sums(field, z + p, xt) for p in range(BY_DOT, GROUP)}
+
+                def piece(p, yt, part):
+                    return have[pl.ds((p * yt_n + yt) * nx + xt * SUB, SUB), pl.ds(part * LANES, LANES)]
+                outer = {(p, yt): piece(p, yt, 1) for p in range(BY_DOT) for yt in range(yt_n)}
                 for yt in range(yt_n):
-                    emit(z, xt, yt, *center_and_lap(field, z, xt, yt, sums[yt]))
-                sums = ahead
+                    at = (z + 1) * plane + SUB + xt * SUB + yt * pitch
+                    mid = [field[pl.ds(at + (p - 1) * plane, SUB), :] for p in range(GROUP + 2)]
+                    for p in range(GROUP):
+                        x_sum = field[pl.ds(at + p * plane + 1, SUB), :] + field[pl.ds(at + p * plane - 1, SUB), :]
+                        if p < BY_DOT:
+                            y_sum = piece(p, yt, 0) + jnp.where(
+                                lower_half, outer.get((p, yt - 1), zero), outer.get((p, yt + 1), zero))
+                        else:
+                            y_sum = rolled[p][yt]
+                        lap = ((mid[p] + mid[p + 2]) + x_sum) + y_sum - 6.0 * mid[p + 1]
+                        emit(z + p, xt, yt, mid[p + 1], lap)
             if out is not None:
-                pack_edges(out, stage_out, z)
-            return sums
-
-        def one_chunk(k, sums):
+                for p in range(GROUP):
+                    pack_edges(out, stage_out, z + p)
+
+        dot_sums(field, 0, dots_a)
+
+        @pl.loop(0, chunks)
+        def _(k):
             before(k)
             wait_halo(stage_in, k)
-            sums = lax.fori_loop(0, CHUNK, lambda i, c: one_plane(k * CHUNK + i, c), sums, unroll=UNROLL)
+
+            @pl.loop(0, CHUNK // GROUP // 2)
+            def _(i):
+                g = k * (CHUNK // GROUP) + 2 * i
+                one_group(g, dots_a, dots_b)
+                one_group(g + 1, dots_b, dots_a)
             if out is not None:
                 send_edges(stage_out, k)
             after(k)
-            return sums
-
-        lax.fori_loop(0, chunks, one_chunk, y_sums(field, 0, 0))
 
     def nothing(k):
         pass
@@ -299,6 +334,7 @@
     natural = pltpu.VMEM((cz, nx, ny), f32)
     sheet = pltpu.VMEM((1, nx, ny), f32)
     edges = pltpu.VMEM((4, 2, cz, yt_n, LANES), f32)
+    dots = pltpu.VMEM((BY_DOT * yt_n * nx, 2 * LANES), f32)
     dma = pltpu.SemaphoreType.DMA
     arrays = [pltpu.with_memory_space_constraint(a, pltpu.HBM) for a in (state, coeff, target, control, multiplier)]
     results = pl.pallas_call(
@@ -306,7 +342,7 @@
         out_shape=(natural, natural, sheet, sheet),
         in_specs=[pl.BlockSpec(memory_space=pltpu.HBM)] * 5,
         out_specs=[pl.BlockSpec(memory_space=pltpu.VMEM)] * 4,
-        scratch_shapes=[padded, padded, natural, natural] + [sheet] * 7 + [edges, edges]
+        scratch_shapes=[padded, padded, natural, natural] + [sheet] * 7 + [edges, edges, pltpu.VMEM((2 * LANES, 2 * LANES), jnp.bfloat16), dots, dots]
         + [dma((chunks, yt_n)), dma((chunks,)), dma((chunks,)), dma((2,)),
            dma((4, 2, chunks)), dma((4, 2, chunks)), dma((3,)), dma((3,))],
         compiler_params=pltpu.CompilerParams(

time: 33.6 us -> 32.6 us (0.970)
  Pallas kernels: 32.9 us -> 31.9 us
    pallas_call x1, Pallas kernels: 29.5 us -> 28.4 us  [iterate(): pl.pallas_call(functools.partial(kernel, cz, nx, ny, n_slab, n_tile), out...]
where the time goes in v2:
time: 32.6 us; the launch traced here: 32.5 us
  Pallas kernels  31.9 us (98%)
  between operations  0.64 us (2%)
    pallas_call x1, Pallas kernels, iterate(): pl.pallas_call(functools.partial(kernel, cz, nx, ny, n_slab, n_tile), out...  28.4 us
    pallas_call x1, Pallas kernels, iterate(): pl.pallas_call(functools.partial(write_out, PARTS), out_shape=(full, full...  3.45 us

profile of v2, /device:TPU:32, one launch (start us, length us, event | category | flops | bytes accessed | tf_op | source)
XLA Modules:
  0.0 32.5 jit_solution(18247529958960401597)
XLA Ops:
  0.6 28.4 %shard_map.84 = (f32[64,16,1024]{2,1,0:T(8,128)S(1)}, f32[64,16,1024]{2,1,0:T(8,128)S(1)}, f32[1,16,1024]{2,1,0:T(8,128)S(1)}, f32[1,16,1024]{2,1,0:T(8,128)S(1)}) custom-call(f32[64,16,1024]{2,1,0:T(8,128)} %state.1, f32[64,16,1024]{2,1,0:T(8,128)} %coeff.1, f32[64,16,1024]{2,1,0:T(8,128)} %target.1, f32[1,16,1024]{2,1,0:T(8,128)} %control.1, ...), custom_call_target="tpu_custom_call" | custom-call | tf_op jit(solution)/shard_map/pallas_call | solution.py:340
  29.1 3.4 %shard_map.85 = (f32[64,16,1024]{2,1,0:T(8,128)}, f32[64,16,1024]{2,1,0:T(8,128)}, f32[1,16,1024]{2,1,0:T(8,128)}, f32[1,16,1024]{2,1,0:T(8,128)}) custom-call(f32[64,16,1024]{2,1,0:T(8,128)S(1)} %get-tuple-element.8.refs_0_, f32[64,16,1024]{2,1,0:T(8,128)S(1)} %get-tuple-element.9.refs_1_, f32[1,16,1024]{2,1,0:T(8,128)S(1)} %get-tuple-element.10.refs_2_, ...), custom_call_target="tpu_custom_call" | custom-call | tf_op jit(solution)/shard_map/pallas_call | solution.py:353

commit v3 on v2

--- a/solution.py
+++ b/solution.py
@@ -11,18 +11,21 @@
 tau_step = 0.5
 LANES = 128
 SUB = 8
-CHUNK = 16
+CHUNK = 8
 GROUP = 4
-BY_DOT = 2
+BY_DOT = 3
 PARTS = 4
+UNITS = 2
+NY = 1024
+NX_LOCAL = 16
 MESH = pl.DeviceIdType.MESH
 
 
-def kernel(cz, nx, ny, n_slab, n_tile,
+def kernel(cz, nx, ny, n_slab, n_tile, accumulators,
            state, coeff, target, control, multiplier,
            final, adj, new_control, new_multiplier,
            sp, mp, cf, tg, above, mult, below, flux, top_two, low_trace, low_flux,
-           send, recv, band, dots_a, dots_b,
+           send, recv, band,
            sem_state, sem_coeff, sem_target, sem_small, sem_send, sem_recv, sem_slab_send, sem_slab_recv):
     yt_n = ny // LANES
     xt_n = nx // SUB
@@ -147,18 +150,27 @@
     swap = jnp.logical_or(jnp.logical_and(row == LANES - 1, col == 0), jnp.logical_and(row == 0, col == LANES - 1))
     band[:, pl.ds(0, LANES)] = jnp.where(jnp.abs(row - col) == 1, 1.0, 0.0).astype(jnp.bfloat16)
     band[:, pl.ds(LANES, LANES)] = jnp.where(swap, 1.0, 0.0).astype(jnp.bfloat16)
-    lower_half = lane < LANES // 2
-
-    def dot_sums(field, z, to):
-        rows = []
+    lower_half = lax.broadcasted_iota(jnp.int32, (nx, LANES), 1) < LANES // 2
+    no_piece = jnp.zeros((nx, LANES), jnp.float32)
+
+    def start_dots(field, z, accs, load=False):
         for p in range(BY_DOT):
             base = (z + p + 1) * plane + SUB
             for yt in range(yt_n):
                 mid = field[pl.ds(base + yt * pitch, nx), :]
                 high = mid.astype(jnp.bfloat16)
                 low = (mid - high.astype(jnp.float32)).astype(jnp.bfloat16)
-                rows.append(jnp.concatenate([high, low], axis=1))
-        to[...] = jnp.dot(jnp.concatenate(rows, axis=0), band[...], preferred_element_type=jnp.float32)
+                pltpu.matmul_acc_lhs(accs[p * yt_n + yt], jnp.concatenate([high, low], axis=1),
+                                     load_staged_rhs=0 if load and p * yt_n + yt < UNITS else None)
+
+    def take_dots(accs, p):
+        both = [pltpu.matmul_pop(accs[p * yt_n + yt]) for yt in range(yt_n)]
+        sums = []
+        for yt in range(yt_n):
+            lower = both[yt - 1][:, LANES:] if yt else no_piece
+            upper = both[yt + 1][:, LANES:] if yt + 1 < yt_n else no_piece
+            sums.append(both[yt][:, :LANES] + jnp.where(lower_half, lower, upper))
+        return [[v[xt * SUB:(xt + 1) * SUB] for v in sums] for xt in range(xt_n)]
 
     def put(field, z, xt, yt, value):
         field[pl.ds((z + 1) * plane + SUB + xt * SUB + yt * pitch, SUB), :] = value
@@ -173,44 +185,47 @@
             z = g * GROUP
             for p in range(GROUP):
                 place_halo(field, stage_in, z + p)
-            dot_sums(field, lax.rem(g + 1, groups) * GROUP, make)
-            for xt in range(xt_n):
-                rolled = {p: y_sums(field, z + p, xt) for p in range(BY_DOT, GROUP)}
-
-                def piece(p, yt, part):
-                    return have[pl.ds((p * yt_n + yt) * nx + xt * SUB, SUB), pl.ds(part * LANES, LANES)]
-                outer = {(p, yt): piece(p, yt, 1) for p in range(BY_DOT) for yt in range(yt_n)}
+            start_dots(field, lax.rem(g + 1, groups) * GROUP, make)
+            for p in range(GROUP):
+                if p < BY_DOT:
+                    sums = take_dots(have, p)
+                else:
+                    sums = [y_sums(field, z + p, xt) for xt in range(xt_n)]
                 for yt in range(yt_n):
-                    at = (z + 1) * plane + SUB + xt * SUB + yt * pitch
-                    mid = [field[pl.ds(at + (p - 1) * plane, SUB), :] for p in range(GROUP + 2)]
-                    for p in range(GROUP):
-                        x_sum = field[pl.ds(at + p * plane + 1, SUB), :] + field[pl.ds(at + p * plane - 1, SUB), :]
-                        if p < BY_DOT:
-                            y_sum = piece(p, yt, 0) + jnp.where(
-                                lower_half, outer.get((p, yt - 1), zero), outer.get((p, yt + 1), zero))
-                        else:
-                            y_sum = rolled[p][yt]
-                        lap = ((mid[p] + mid[p + 2]) + x_sum) + y_sum - 6.0 * mid[p + 1]
-                        emit(z + p, xt, yt, mid[p + 1], lap)
+                    for xt in range(xt_n):
+                        at = (z + p + 1) * plane + SUB + xt * SUB + yt * pitch
+                        mid = field[pl.ds(at, SUB), :]
+                        x_sum = field[pl.ds(at + 1, SUB), :] + field[pl.ds(at - 1, SUB), :]
+                        z_sum = field[pl.ds(at + plane, SUB), :] + field[pl.ds(at - plane, SUB), :]
+                        emit(z + p, xt, yt, mid, (z_sum + x_sum) + sums[xt][yt] - 6.0 * mid)
             if out is not None:
                 for p in range(GROUP):
                     pack_edges(out, stage_out, z + p)
 
-        dot_sums(field, 0, dots_a)
-
-        @pl.loop(0, chunks)
-        def _(k):
-            before(k)
-            wait_halo(stage_in, k)
-
-            @pl.loop(0, CHUNK // GROUP // 2)
-            def _(i):
-                g = k * (CHUNK // GROUP) + 2 * i
-                one_group(g, dots_a, dots_b)
-                one_group(g + 1, dots_b, dots_a)
-            if out is not None:
-                send_edges(stage_out, k)
-            after(k)
+        def with_accumulators(*accs):
+            first, second = accs[:BY_DOT * yt_n], accs[BY_DOT * yt_n:]
+            for unit in range(UNITS):
+                pltpu.matmul_push_rhs(band[...], 0, unit)
+            start_dots(field, 0, first, True)
+
+            @pl.loop(0, chunks)
+            def _(k):
+                before(k)
+                wait_halo(stage_in, k)
+
+                @pl.loop(0, CHUNK // GROUP // 2)
+                def _(i):
+                    g = k * (CHUNK // GROUP) + 2 * i
+                    one_group(g, first, second)
+                    one_group(g + 1, second, first)
+                if out is not None:
+                    send_edges(stage_out, k)
+                after(k)
+
+            for acc in first:
+                pltpu.matmul_pop(acc)
+
+        pl.run_scoped(with_accumulators, *accumulators)
 
     def nothing(k):
         pass
@@ -325,7 +340,7 @@
         copy.wait()
 
 
-def iterate(n_slab, n_tile, state, coeff, target, control, multiplier):
+def iterate(n_slab, n_tile, accumulators, state, coeff, target, control, multiplier):
     cz, nx, ny = state.shape
     yt_n = ny // LANES
     chunks = cz // CHUNK
@@ -334,15 +349,14 @@
     natural = pltpu.VMEM((cz, nx, ny), f32)
     sheet = pltpu.VMEM((1, nx, ny), f32)
     edges = pltpu.VMEM((4, 2, cz, yt_n, LANES), f32)
-    dots = pltpu.VMEM((BY_DOT * yt_n * nx, 2 * LANES), f32)
     dma = pltpu.SemaphoreType.DMA
     arrays = [pltpu.with_memory_space_constraint(a, pltpu.HBM) for a in (state, coeff, target, control, multiplier)]
     results = pl.pallas_call(
-        functools.partial(kernel, cz, nx, ny, n_slab, n_tile),
+        functools.partial(kernel, cz, nx, ny, n_slab, n_tile, accumulators),
         out_shape=(natural, natural, sheet, sheet),
         in_specs=[pl.BlockSpec(memory_space=pltpu.HBM)] * 5,
         out_specs=[pl.BlockSpec(memory_space=pltpu.VMEM)] * 4,
-        scratch_shapes=[padded, padded, natural, natural] + [sheet] * 7 + [edges, edges, pltpu.VMEM((2 * LANES, 2 * LANES), jnp.bfloat16), dots, dots]
+        scratch_shapes=[padded, padded, natural, natural] + [sheet] * 7 + [edges, edges, pltpu.VMEM((2 * LANES, 2 * LANES), jnp.bfloat16)]
         + [dma((chunks, yt_n)), dma((chunks,)), dma((chunks,)), dma((2,)),
            dma((4, 2, chunks)), dma((4, 2, chunks)), dma((3,)), dma((3,))],
         compiler_params=pltpu.CompilerParams(
@@ -362,5 +376,8 @@
 
 def solution(mesh):
     spec = P("slab", "tile", None)
-    run = functools.partial(iterate, mesh.shape["slab"], mesh.shape["tile"])
+    with jax.sharding.use_abstract_mesh(mesh.abstract_mesh):
+        count = 2 * BY_DOT * (NY // LANES)
+        accumulators = [pltpu.ACC(mxu_id=i % UNITS)((NX_LOCAL, 2 * LANES), jnp.float32) for i in range(count)]
+    run = functools.partial(iterate, mesh.shape["slab"], mesh.shape["tile"], accumulators)
     return jax.shard_map(run, mesh=mesh, in_specs=(spec,) * 5, out_specs=(spec,) * 4, check_vma=False)

time: 32.6 us -> 31.6 us (0.969)
  Pallas kernels: 31.9 us -> 30.8 us
    pallas_call x1, Pallas kernels: 28.4 us -> 27.4 us  [iterate(): pl.pallas_call(functools.partial(kernel, cz, nx, ny, n_slab, n_tile, accu...]
where the time goes in v3:
time: 31.6 us; the launch traced here: 31.4 us
  Pallas kernels  30.8 us (97%)
  between operations  0.64 us (2%)
    pallas_call x1, Pallas kernels, iterate(): pl.pallas_call(functools.partial(kernel, cz, nx, ny, n_slab, n_tile, accu...  27.4 us
    pallas_call x1, Pallas kernels, iterate(): pl.pallas_call(functools.partial(write_out, PARTS), out_shape=(full, full...  3.45 us

profile of v3, /device:TPU:32, one launch (start us, length us, event | category | flops | bytes accessed | tf_op | source)
XLA Modules:
  0.0 31.4 jit_solution(6194452487164824560)
XLA Ops:
  0.6 27.4 %shard_map.84 = (f32[64,16,1024]{2,1,0:T(8,128)S(1)}, f32[64,16,1024]{2,1,0:T(8,128)S(1)}, f32[1,16,1024]{2,1,0:T(8,128)S(1)}, f32[1,16,1024]{2,1,0:T(8,128)S(1)}) custom-call(f32[64,16,1024]{2,1,0:T(8,128)} %state.1, f32[64,16,1024]{2,1,0:T(8,128)} %coeff.1, f32[64,16,1024]{2,1,0:T(8,128)} %target.1, f32[1,16,1024]{2,1,0:T(8,128)} %control.1, ...), custom_call_target="tpu_custom_call" | custom-call | tf_op jit(solution)/shard_map/pallas_call | solution.py:354
  28.0 3.4 %shard_map.85 = (f32[64,16,1024]{2,1,0:T(8,128)}, f32[64,16,1024]{2,1,0:T(8,128)}, f32[1,16,1024]{2,1,0:T(8,128)}, f32[1,16,1024]{2,1,0:T(8,128)}) custom-call(f32[64,16,1024]{2,1,0:T(8,128)S(1)} %get-tuple-element.8.refs_0_, f32[64,16,1024]{2,1,0:T(8,128)S(1)} %get-tuple-element.9.refs_1_, f32[1,16,1024]{2,1,0:T(8,128)S(1)} %get-tuple-element.10.refs_2_, ...), custom_call_target="tpu_custom_call" | custom-call | tf_op jit(solution)/shard_map/pallas_call | solution.py:367

commit v4 on v1

--- a/solution.py
+++ b/solution.py
@@ -11,17 +11,124 @@
 tau_step = 0.5
 LANES = 128
 SUB = 8
-CHUNK = 16
-UNROLL = 4
-PARTS = 4
+CHUNK = 8
+GROUP = 4
+BY_DOT = 3
+UNITS = 2
+NY = 1024
+NX_LOCAL = 16
 MESH = pl.DeviceIdType.MESH
 
 
-def kernel(cz, nx, ny, n_slab, n_tile,
+def nothing(_):
+    pass
+
+
+def tools(cz, nx, ny, accumulators, band):
+    yt_n = ny // LANES
+    xt_n = nx // SUB
+    pitch = nx + SUB
+    plane = yt_n * pitch
+    chunks = cz // CHUNK
+    lane = lax.broadcasted_iota(jnp.int32, (SUB, LANES), 1)
+    first = lane == 0
+    last = lane == LANES - 1
+    zero = jnp.zeros((SUB, LANES), jnp.float32)
+
+    def y_sums(field, z, xt):
+        base = (z + 1) * plane + SUB + xt * SUB
+        mid = [field[pl.ds(base + yt * pitch, SUB), :] for yt in range(yt_n)]
+        right = [pltpu.roll(v, 1, 1) for v in mid]
+        left = [pltpu.roll(v, LANES - 1, 1) for v in mid]
+        return [jnp.where(first, right[yt - 1] if yt else zero, right[yt])
+                + jnp.where(last, left[yt + 1] if yt + 1 < yt_n else zero, left[yt]) for yt in range(yt_n)]
+
+    row = lax.rem(lax.broadcasted_iota(jnp.int32, (2 * LANES, LANES), 0), LANES)
+    col = lax.broadcasted_iota(jnp.int32, (2 * LANES, LANES), 1)
+    swap = jnp.logical_or(jnp.logical_and(row == LANES - 1, col == 0), jnp.logical_and(row == 0, col == LANES - 1))
+    band[:, pl.ds(0, LANES)] = jnp.where(jnp.abs(row - col) == 1, 1.0, 0.0).astype(jnp.bfloat16)
+    band[:, pl.ds(LANES, LANES)] = jnp.where(swap, 1.0, 0.0).astype(jnp.bfloat16)
+    lower_half = lax.broadcasted_iota(jnp.int32, (nx, LANES), 1) < LANES // 2
+    no_piece = jnp.zeros((nx, LANES), jnp.float32)
+
+    def start_dots(field, z, accs, load=False):
+        for p in range(BY_DOT):
+            base = (z + p + 1) * plane + SUB
+            for yt in range(yt_n):
+                mid = field[pl.ds(base + yt * pitch, nx), :]
+                high = mid.astype(jnp.bfloat16)
+                low = (mid - high.astype(jnp.float32)).astype(jnp.bfloat16)
+                pltpu.matmul_acc_lhs(accs[p * yt_n + yt], jnp.concatenate([high, low], axis=1),
+                                     load_staged_rhs=0 if load and p * yt_n + yt < UNITS else None)
+
+    def take_dots(accs, p):
+        both = [pltpu.matmul_pop(accs[p * yt_n + yt]) for yt in range(yt_n)]
+        sums = []
+        for yt in range(yt_n):
+            lower = both[yt - 1][:, LANES:] if yt else no_piece
+            upper = both[yt + 1][:, LANES:] if yt + 1 < yt_n else no_piece
+            sums.append(both[yt][:, :LANES] + jnp.where(lower_half, lower, upper))
+        return [[v[xt * SUB:(xt + 1) * SUB] for v in sums] for xt in range(xt_n)]
+
+    def put(field, z, xt, yt, value):
+        field[pl.ds((z + 1) * plane + SUB + xt * SUB + yt * pitch, SUB), :] = value
+
+    def at(xt, yt):
+        return pl.ds(xt * SUB, SUB), pl.ds(yt * LANES, LANES)
+
+    groups = cz // GROUP
+
+    def sweep(field, emit, before, after, place=nothing, pack=nothing):
+        def one_group(g, have, make):
+            z = g * GROUP
+            for p in range(GROUP):
+                place(z + p)
+            start_dots(field, lax.rem(g + 1, groups) * GROUP, make)
+            for p in range(GROUP):
+                if p < BY_DOT:
+                    sums = take_dots(have, p)
+                else:
+                    sums = [y_sums(field, z + p, xt) for xt in range(xt_n)]
+                for yt in range(yt_n):
+                    for xt in range(xt_n):
+                        at = (z + p + 1) * plane + SUB + xt * SUB + yt * pitch
+                        mid = field[pl.ds(at, SUB), :]
+                        x_sum = field[pl.ds(at + 1, SUB), :] + field[pl.ds(at - 1, SUB), :]
+                        z_sum = field[pl.ds(at + plane, SUB), :] + field[pl.ds(at - plane, SUB), :]
+                        emit(z + p, xt, yt, mid, (z_sum + x_sum) + sums[xt][yt] - 6.0 * mid)
+            for p in range(GROUP):
+                pack(z + p)
+
+        def with_accumulators(*accs):
+            first, second = accs[:BY_DOT * yt_n], accs[BY_DOT * yt_n:]
+            for unit in range(UNITS):
+                pltpu.matmul_push_rhs(band[...], 0, unit)
+            start_dots(field, 0, first, True)
+
+            @pl.loop(0, chunks)
+            def _(k):
+                before(k)
+
+                @pl.loop(0, CHUNK // GROUP // 2)
+                def _(i):
+                    g = k * (CHUNK // GROUP) + 2 * i
+                    one_group(g, first, second)
+                    one_group(g + 1, second, first)
+                after(k)
+
+            for acc in first:
+                pltpu.matmul_pop(acc)
+
+        pl.run_scoped(with_accumulators, *accumulators)
+
+    return sweep, put, at, zero
+
+
+def kernel(cz, nx, ny, n_slab, n_tile, accumulators,
            state, coeff, target, control, multiplier,
-           final, adj, new_control, new_multiplier,
-           sp, mp, cf, tg, above, mult, below, flux, top_two, low_trace, low_flux,
-           send, recv,
+           final, tg, mp, new_control, new_multiplier,
+           sp, cf, above, mult, below, flux, top_two, low_trace, low_flux,
+           send, recv, band,
            sem_state, sem_coeff, sem_target, sem_small, sem_send, sem_recv, sem_slab_send, sem_slab_recv):
     yt_n = ny // LANES
     xt_n = nx // SUB
@@ -103,7 +210,13 @@
         return pltpu.make_async_remote_copy(
             src_ref=send.at[stage, side, pl.ds(k * CHUNK, CHUNK)],
             dst_ref=recv.at[stage, 1 - side, pl.ds(k * CHUNK, CHUNK)],
-            send_sem=sem_send.at[stage, side, k], recv_sem=sem_recv.at[stage, 1 - side, k],
+            send_sem=sem_send.at[stage, side], recv_sem=sem_recv.at[stage, 1 - side, k],
+            device_id=side_dev[side], device_id_type=MESH)
+
+    def all_edges(stage, side):
+        return pltpu.make_async_remote_copy(
+            src_ref=send.at[stage, side], dst_ref=recv.at[stage, 1 - side],
+            send_sem=sem_send.at[stage, side], recv_sem=sem_recv.at[stage, 1 - side, 0],
             device_id=side_dev[side], device_id_type=MESH)
 
     def pack_edges(field, stage, z):
@@ -123,62 +236,22 @@
             def _():
                 edge_copy(stage, 1 - side, k).wait_recv()
 
+    def stage(field, number, emit, out, before=nothing, after=nothing):
+        def start(k):
+            before(k)
+            wait_halo(number, k)
+
+        def end(k):
+            send_edges(number + 1, k)
+            after(k)
+        sweep(field, emit, start, end, lambda z: place_halo(field, number, z), lambda z: pack_edges(out, number + 1, z))
+
     def place_halo(field, stage, z):
         base = (z + 1) * plane
         field[pl.ds(base + SUB - 1, yt_n, stride=pitch), :] = recv[stage, 0, z]
         field[pl.ds(base + SUB + nx, yt_n, stride=pitch), :] = recv[stage, 1, z]
 
-    lane = lax.broadcasted_iota(jnp.int32, (SUB, LANES), 1)
-    first = lane == 0
-    last = lane == LANES - 1
-    zero = jnp.zeros((SUB, LANES), jnp.float32)
-
-    def y_sums(field, z, xt):
-        base = (z + 1) * plane + SUB + xt * SUB
-        mid = [field[pl.ds(base + yt * pitch, SUB), :] for yt in range(yt_n)]
-        right = [pltpu.roll(v, 1, 1) for v in mid]
-        left = [pltpu.roll(v, LANES - 1, 1) for v in mid]
-        return [jnp.where(first, right[yt - 1] if yt else zero, right[yt])
-                + jnp.where(last, left[yt + 1] if yt + 1 < yt_n else zero, left[yt]) for yt in range(yt_n)]
-
-    def center_and_lap(field, z, xt, yt, y_sum):
-        at = (z + 1) * plane + SUB + xt * SUB + yt * pitch
-        mid = field[pl.ds(at, SUB), :]
-        z_sum = field[pl.ds(at + plane, SUB), :] + field[pl.ds(at - plane, SUB), :]
-        x_sum = field[pl.ds(at + 1, SUB), :] + field[pl.ds(at - 1, SUB), :]
-        return mid, (z_sum + x_sum) + y_sum - 6.0 * mid
-
-    def put(field, z, xt, yt, value):
-        field[pl.ds((z + 1) * plane + SUB + xt * SUB + yt * pitch, SUB), :] = value
-
-    def at(xt, yt):
-        return pl.ds(xt * SUB, SUB), pl.ds(yt * LANES, LANES)
-
-    def sweep(field, stage_in, emit, before, after, out=None, stage_out=None):
-        def one_plane(z, sums):
-            place_halo(field, stage_in, z)
-            for xt in range(xt_n):
-                ahead = y_sums(field, z, xt + 1) if xt + 1 < xt_n else y_sums(field, z + 1, 0)
-                for yt in range(yt_n):
-                    emit(z, xt, yt, *center_and_lap(field, z, xt, yt, sums[yt]))
-                sums = ahead
-            if out is not None:
-                pack_edges(out, stage_out, z)
-            return sums
-
-        def one_chunk(k, sums):
-            before(k)
-            wait_halo(stage_in, k)
-            sums = lax.fori_loop(0, CHUNK, lambda i, c: one_plane(k * CHUNK + i, c), sums, unroll=UNROLL)
-            if out is not None:
-                send_edges(stage_out, k)
-            after(k)
-            return sums
-
-        lax.fori_loop(0, chunks, one_chunk, y_sums(field, 0, 0))
-
-    def nothing(k):
-        pass
+    sweep, put, at, zero = tools(cz, nx, ny, accumulators, band)
 
     @pl.loop(0, chunks)
     def _(k):
@@ -203,7 +276,7 @@
     def middle(z, xt, yt, mid, lap):
         put(m2, z, xt, yt, mid + cf[(z,) + at(xt, yt)] * lap)
 
-    sweep(s2, 0, middle, lambda k: coeff_copy(k).wait(), nothing, m2, 1)
+    stage(s2, 0, middle, m2, lambda k: coeff_copy(k).wait())
 
     for xt in range(xt_n):
         for yt in range(yt_n):
@@ -224,7 +297,7 @@
         def _():
             trace_copy.start()
 
-    sweep(m2, 1, finish, lambda k: target_copy(k).wait(), send_trace, s2, 2)
+    stage(m2, 1, finish, s2, lambda k: target_copy(k).wait(), send_trace)
 
     for xt in range(xt_n):
         for yt in range(yt_n):
@@ -246,13 +319,7 @@
             flux[0] = cf[0] * (tg[0] + flux[0])
             flux_copy.start()
 
-    sweep(s2, 2, back_one, nothing, send_flux, m2, 3)
-
-    def back_two(z, xt, yt, mid, lap):
-        here = (z,) + at(xt, yt)
-        adj[here] = tg[here] + lap
-
-    sweep(m2, 3, back_two, nothing, nothing)
+    stage(s2, 2, back_one, m2, nothing, send_flux)
 
     mult_copy.wait()
     trace_copy.wait_recv()
@@ -265,32 +332,47 @@
     below_copy.wait_send()
     trace_copy.wait_send()
     flux_copy.wait_send()
+    @pl.loop(0, chunks)
+    def _(k):
+        wait_halo(3, k)
+        for i in range(CHUNK):
+            place_halo(m2, 3, k * CHUNK + i)
+
     for side in range(2):
         @pl.when(has[side])
         def _():
-            for stage in range(4):
-                @pl.loop(0, chunks)
-                def _(k):
-                    edge_copy(stage, side, k).wait_send()
-
-
-def write_out(parts, *refs):
-    sem = refs[-1]
-    n = (len(refs) - 1) // 2
-    copies = []
-    for i in range(n):
-        planes = refs[i].shape[0]
-        step = max(planes // parts, 1)
-        for j in range(planes // step):
-            span = pl.ds(j * step, step)
-            copies.append(pltpu.make_async_copy(refs[i].at[span], refs[n + i].at[span], sem.at[i, j]))
+            for number in range(4):
+                all_edges(number, side).wait_send()
+
+
+def last_stage(cz, nx, ny, accumulators,
+               final, tg, mp, control, multiplier, final_out, adj_out, control_out, multiplier_out,
+               adj, band, sem, sem_adj):
+    copies = [pltpu.make_async_copy(a, b, sem.at[i]) for i, (a, b) in enumerate(
+        ((final, final_out), (control, control_out), (multiplier, multiplier_out)))]
     for copy in copies:
         copy.start()
+    m2 = mp.reshape(mp.shape[0] * (ny // LANES) * (nx + SUB), LANES)
+    sweep, _, at, _ = tools(cz, nx, ny, accumulators, band)
+
+    def adj_copy(k):
+        planes = pl.ds(k * CHUNK, CHUNK)
+        return pltpu.make_async_copy(adj.at[planes], adj_out.at[planes], sem_adj.at[k])
+
+    def back_two(z, xt, yt, mid, lap):
+        here = (z,) + at(xt, yt)
+        adj[here] = tg[here] + lap
+
+    sweep(m2, back_two, nothing, lambda k: adj_copy(k).start())
     for copy in copies:
         copy.wait()
 
-
-def iterate(n_slab, n_tile, state, coeff, target, control, multiplier):
+    @pl.loop(0, cz // CHUNK)
+    def _(k):
+        adj_copy(k).wait()
+
+
+def iterate(n_slab, n_tile, accumulators, state, coeff, target, control, multiplier):
     cz, nx, ny = state.shape
     yt_n = ny // LANES
     chunks = cz // CHUNK
@@ -302,29 +384,32 @@
     dma = pltpu.SemaphoreType.DMA
     arrays = [pltpu.with_memory_space_constraint(a, pltpu.HBM) for a in (state, coeff, target, control, multiplier)]
     results = pl.pallas_call(
-        functools.partial(kernel, cz, nx, ny, n_slab, n_tile),
-        out_shape=(natural, natural, sheet, sheet),
+        functools.partial(kernel, cz, nx, ny, n_slab, n_tile, accumulators),
+        out_shape=(natural, natural, padded, sheet, sheet),
         in_specs=[pl.BlockSpec(memory_space=pltpu.HBM)] * 5,
-        out_specs=[pl.BlockSpec(memory_space=pltpu.VMEM)] * 4,
-        scratch_shapes=[padded, padded, natural, natural] + [sheet] * 7 + [edges, edges]
+        out_specs=[pl.BlockSpec(memory_space=pltpu.VMEM)] * 5,
+        scratch_shapes=[padded, natural] + [sheet] * 7 + [edges, edges, pltpu.VMEM((2 * LANES, 2 * LANES), jnp.bfloat16)]
         + [dma((chunks, yt_n)), dma((chunks,)), dma((chunks,)), dma((2,)),
-           dma((4, 2, chunks)), dma((4, 2, chunks)), dma((3,)), dma((3,))],
+           dma((4, 2)), dma((4, 2, chunks)), dma((3,)), dma((3,))],
         compiler_params=pltpu.CompilerParams(
-            collective_id=0, has_side_effects=True, vmem_limit_bytes=40 * 2**20),
+            collective_id=0, has_side_effects=True, vmem_limit_bytes=32 * 2**20),
     )(*arrays)
     full = jax.ShapeDtypeStruct((cz, nx, ny), f32)
     face = jax.ShapeDtypeStruct((1, nx, ny), f32)
     return pl.pallas_call(
-        functools.partial(write_out, PARTS),
+        functools.partial(last_stage, cz, nx, ny, accumulators),
         out_shape=(full, full, face, face),
-        in_specs=[pl.BlockSpec(memory_space=pltpu.VMEM)] * 4,
+        in_specs=[pl.BlockSpec(memory_space=pltpu.VMEM)] * 5,
         out_specs=[pl.BlockSpec(memory_space=pl.ANY)] * 4,
-        scratch_shapes=[dma((4, PARTS))],
+        scratch_shapes=[natural, pltpu.VMEM((2 * LANES, 2 * LANES), jnp.bfloat16), dma((3,)), dma((chunks,))],
         compiler_params=pltpu.CompilerParams(vmem_limit_bytes=16 * 2**20),
     )(*results)
 
 
 def solution(mesh):
     spec = P("slab", "tile", None)
-    run = functools.partial(iterate, mesh.shape["slab"], mesh.shape["tile"])
+    with jax.sharding.use_abstract_mesh(mesh.abstract_mesh):
+        count = 2 * BY_DOT * (NY // LANES)
+        accumulators = [pltpu.ACC(mxu_id=i % UNITS)((NX_LOCAL, 2 * LANES), jnp.float32) for i in range(count)]
+    run = functools.partial(iterate, mesh.shape["slab"], mesh.shape["tile"], accumulators)
     return jax.shard_map(run, mesh=mesh, in_specs=(spec,) * 5, out_specs=(spec,) * 4, check_vma=False)

time: 33.6 us -> 30.2 us (0.90)
  Pallas kernels: 32.9 us -> 29.5 us
    pallas_call x2, Pallas kernels: 32.9 us -> 29.5 us  [the longest x1 26.1 us: iterate(): pl.pallas_call(functools.partial(kernel, cz, nx, ny, n_slab, n_tile, accu...]
where the time goes in v4:
time: 30.2 us; the launch traced here: 30.1 us
  Pallas kernels  29.5 us (98%)
  between operations  0.64 us (2%)
    pallas_call x1, Pallas kernels, iterate(): pl.pallas_call(functools.partial(kernel, cz, nx, ny, n_slab, n_tile, accu...  26.1 us
    pallas_call x1, Pallas kernels, iterate(): pl.pallas_call(functools.partial(last_stage, cz, nx, ny, accumulators), o...  3.42 us

profile of v4, /device:TPU:32, one launch (start us, length us, event | category | flops | bytes accessed | tf_op | source)
XLA Modules:
  0.0 30.1 jit_solution(9331792792620751390)
XLA Ops:
  0.6 26.1 %shard_map.84 = (f32[64,16,1024]{2,1,0:T(8,128)S(1)}, f32[64,16,1024]{2,1,0:T(8,128)S(1)}, f32[67,8,24,128]{3,2,1,0:T(8,128)S(1)}, f32[1,16,1024]{2,1,0:T(8,128)S(1)}, f32[1,16,1024]{2,1,0:T(8,128)S(1)}) custom-call(f32[64,16,1024]{2,1,0:T(8,128)} %state.1, f32[64,16,1024]{2,1,0:T(8,128)} %coeff.1, f32[64,16,1024]{2,1,0:T(8,128)} %target.1, ...), custom_call_target="tpu_custom_call" | custom-call | tf_op jit(solution)/shard_map/pallas_call | solution.py:386
  26.7 3.4 %shard_map.85 = (f32[64,16,1024]{2,1,0:T(8,128)}, f32[64,16,1024]{2,1,0:T(8,128)}, f32[1,16,1024]{2,1,0:T(8,128)}, f32[1,16,1024]{2,1,0:T(8,128)}) custom-call(f32[64,16,1024]{2,1,0:T(8,128)S(1)} %get-tuple-element.9.final, f32[64,16,1024]{2,1,0:T(8,128)S(1)} %get-tuple-element.10.tg, f32[67,8,24,128]{3,2,1,0:T(8,128)S(1)} %get-tuple-element.11.mp, ...), custom_call_target="tpu_custom_call" | custom-call | tf_op jit(solution)/shard_map/pallas_call | solution.py:399

commit v5 on v4

--- a/solution.py
+++ b/solution.py
@@ -13,7 +13,6 @@
 SUB = 8
 CHUNK = 8
 GROUP = 4
-BY_DOT = 3
 UNITS = 2
 NY = 1024
 NX_LOCAL = 16
@@ -30,18 +29,7 @@
     pitch = nx + SUB
     plane = yt_n * pitch
     chunks = cz // CHUNK
-    lane = lax.broadcasted_iota(jnp.int32, (SUB, LANES), 1)
-    first = lane == 0
-    last = lane == LANES - 1
     zero = jnp.zeros((SUB, LANES), jnp.float32)
-
-    def y_sums(field, z, xt):
-        base = (z + 1) * plane + SUB + xt * SUB
-        mid = [field[pl.ds(base + yt * pitch, SUB), :] for yt in range(yt_n)]
-        right = [pltpu.roll(v, 1, 1) for v in mid]
-        left = [pltpu.roll(v, LANES - 1, 1) for v in mid]
-        return [jnp.where(first, right[yt - 1] if yt else zero, right[yt])
-                + jnp.where(last, left[yt + 1] if yt + 1 < yt_n else zero, left[yt]) for yt in range(yt_n)]
 
     row = lax.rem(lax.broadcasted_iota(jnp.int32, (2 * LANES, LANES), 0), LANES)
     col = lax.broadcasted_iota(jnp.int32, (2 * LANES, LANES), 1)
@@ -52,7 +40,7 @@
     no_piece = jnp.zeros((nx, LANES), jnp.float32)
 
     def start_dots(field, z, accs, load=False):
-        for p in range(BY_DOT):
+        for p in range(GROUP):
             base = (z + p + 1) * plane + SUB
             for yt in range(yt_n):
                 mid = field[pl.ds(base + yt * pitch, nx), :]
@@ -62,13 +50,13 @@
                                      load_staged_rhs=0 if load and p * yt_n + yt < UNITS else None)
 
     def take_dots(accs, p):
-        both = [pltpu.matmul_pop(accs[p * yt_n + yt]) for yt in range(yt_n)]
-        sums = []
-        for yt in range(yt_n):
-            lower = both[yt - 1][:, LANES:] if yt else no_piece
-            upper = both[yt + 1][:, LANES:] if yt + 1 < yt_n else no_piece
-            sums.append(both[yt][:, :LANES] + jnp.where(lower_half, lower, upper))
-        return [[v[xt * SUB:(xt + 1) * SUB] for v in sums] for xt in range(xt_n)]
+        before, here = no_piece, pltpu.matmul_pop(accs[p * yt_n])
+        for yt in range(yt_n):
+            behind = pltpu.matmul_pop(accs[p * yt_n + yt + 1]) if yt + 1 < yt_n else None
+            upper = no_piece if behind is None else behind[:, LANES:]
+            sums = here[:, :LANES] + jnp.where(lower_half, before, upper)
+            yield [sums[xt * SUB:(xt + 1) * SUB] for xt in range(xt_n)]
+            before, here = here[:, LANES:], behind
 
     def put(field, z, xt, yt, value):
         field[pl.ds((z + 1) * plane + SUB + xt * SUB + yt * pitch, SUB), :] = value
@@ -85,22 +73,18 @@
                 place(z + p)
             start_dots(field, lax.rem(g + 1, groups) * GROUP, make)
             for p in range(GROUP):
-                if p < BY_DOT:
-                    sums = take_dots(have, p)
-                else:
-                    sums = [y_sums(field, z + p, xt) for xt in range(xt_n)]
-                for yt in range(yt_n):
+                for yt, sums in enumerate(take_dots(have, p)):
                     for xt in range(xt_n):
                         at = (z + p + 1) * plane + SUB + xt * SUB + yt * pitch
                         mid = field[pl.ds(at, SUB), :]
                         x_sum = field[pl.ds(at + 1, SUB), :] + field[pl.ds(at - 1, SUB), :]
                         z_sum = field[pl.ds(at + plane, SUB), :] + field[pl.ds(at - plane, SUB), :]
-                        emit(z + p, xt, yt, mid, (z_sum + x_sum) + sums[xt][yt] - 6.0 * mid)
+                        emit(z + p, xt, yt, mid, (z_sum + x_sum) + sums[xt] - 6.0 * mid)
             for p in range(GROUP):
                 pack(z + p)
 
         def with_accumulators(*accs):
-            first, second = accs[:BY_DOT * yt_n], accs[BY_DOT * yt_n:]
+            first, second = accs[:GROUP * yt_n], accs[GROUP * yt_n:]
             for unit in range(UNITS):
                 pltpu.matmul_push_rhs(band[...], 0, unit)
             start_dots(field, 0, first, True)
@@ -409,7 +393,7 @@
 def solution(mesh):
     spec = P("slab", "tile", None)
     with jax.sharding.use_abstract_mesh(mesh.abstract_mesh):
-        count = 2 * BY_DOT * (NY // LANES)
+        count = 2 * GROUP * (NY // LANES)
         accumulators = [pltpu.ACC(mxu_id=i % UNITS)((NX_LOCAL, 2 * LANES), jnp.float32) for i in range(count)]
     run = functools.partial(iterate, mesh.shape["slab"], mesh.shape["tile"], accumulators)
     return jax.shard_map(run, mesh=mesh, in_specs=(spec,) * 5, out_specs=(spec,) * 4, check_vma=False)

time: 30.2 us -> 30.1 us (level)
  no operation moved by 1% of the time
where the time goes in v5:
time: 30.1 us; the launch traced here: 30 us
  Pallas kernels  29.4 us (98%)
  between operations  0.64 us (2%)
    pallas_call x1, Pallas kernels, iterate(): pl.pallas_call(functools.partial(kernel, cz, nx, ny, n_slab, n_tile, accu...  26 us
    pallas_call x1, Pallas kernels, iterate(): pl.pallas_call(functools.partial(last_stage, cz, nx, ny, accumulators), o...  3.42 us

profile of v5, /device:TPU:32, one launch (start us, length us, event | category | flops | bytes accessed | tf_op | source)
XLA Modules:
  0.0 30.0 jit_solution(2748372841929790706)
XLA Ops:
  0.6 26.0 %shard_map.84 = (f32[64,16,1024]{2,1,0:T(8,128)S(1)}, f32[64,16,1024]{2,1,0:T(8,128)S(1)}, f32[67,8,24,128]{3,2,1,0:T(8,128)S(1)}, f32[1,16,1024]{2,1,0:T(8,128)S(1)}, f32[1,16,1024]{2,1,0:T(8,128)S(1)}) custom-call(f32[64,16,1024]{2,1,0:T(8,128)} %state.1, f32[64,16,1024]{2,1,0:T(8,128)} %coeff.1, f32[64,16,1024]{2,1,0:T(8,128)} %target.1, ...), custom_call_target="tpu_custom_call" | custom-call | tf_op jit(solution)/shard_map/pallas_call | solution.py:370
  26.6 3.4 %shard_map.85 = (f32[64,16,1024]{2,1,0:T(8,128)}, f32[64,16,1024]{2,1,0:T(8,128)}, f32[1,16,1024]{2,1,0:T(8,128)}, f32[1,16,1024]{2,1,0:T(8,128)}) custom-call(f32[64,16,1024]{2,1,0:T(8,128)S(1)} %get-tuple-element.9.final, f32[64,16,1024]{2,1,0:T(8,128)S(1)} %get-tuple-element.10.tg, f32[67,8,24,128]{3,2,1,0:T(8,128)S(1)} %get-tuple-element.11.mp, ...), custom_call_target="tpu_custom_call" | custom-call | tf_op jit(solution)/shard_map/pallas_call | solution.py:383
